TPU v7x, 256 devices: a whole 4x4x8 slice. The times are simulated.
256 devices in a mesh: block: 8 (over z), tile: 32 (over x, y, core).
Axes of the slice: x: 4, y: 4, z: 8, core: 2. Of those that a mesh axis runs over, the one named last changes fastest.
Arguments:
- acts: bfloat16 [16, 32, 64, 384], P('block', 'tile'), may hold values from -6 to 6
- gamma: float32 [384], replicated, may hold values from 0.25 to 1.75
- beta: float32 [384], replicated, may hold values from -3 to 3
- weights: bfloat16 [384, 27, 192], P('tile'), may hold values from -0.0625 to 0.0625
- cotangent: bfloat16 [16, 64, 128, 192], P('block', 'tile'), may hold values from -6 to 6
Outputs:
- d_acts: bfloat16 [16, 32, 64, 384], P('block', 'tile')
- d_weights: float32 [384, 27, 192], P('tile')
All inputs are finite; a program needn't handle non-finite values.
Results may differ from a plain program's by a relative error of at most 0.0029.
Values may be sent and summed in bfloat16 or wider, within the bound.
A program may use at most 128 MiB of HBM per device.

v0:
```python
import jax
import jax.numpy as jnp
from jax import lax
from jax.sharding import PartitionSpec as P

GROUPS = 32
norm_eps = 1e-06


def from_behind(value, axis, steps):
    count = lax.axis_size(axis)
    first, last = (max(0, -steps), min(count, count - steps))
    return lax.ppermute(value, axis, [(source, source + steps) for source in range(first, last)])


def padded_2(value, sides, width):
    for axis, dim in sides:
        size, length = (lax.axis_size(axis), value.shape[dim])
        up = [(i, (i + 1) % size) for i in range(size - 1)]
        down = [(j, i) for i, j in up]
        last = lax.slice_in_dim(value, length - width, length, axis=dim)
        first = lax.slice_in_dim(value, 0, width, axis=dim)
        before = lax.ppermute(last, axis, up)
        after = lax.ppermute(first, axis, down)
        value = jnp.concatenate([before, value, after], axis=dim)
    return value


def group_totals(values, frames, per_group):
    return jnp.sum(values, axis=(1, 2)).reshape(frames, GROUPS, per_group).sum(-1)


def shards(acts, gamma, beta, weights, cotangent):
    frames, low_rows, low_cols, channels = acts.shape
    tiles = lax.axis_size("tile")
    per_group = channels // GROUPS
    group_size = low_rows * tiles * low_cols * per_group
    acts_wide = acts.astype(jnp.float32)
    stat_sum = group_totals(acts_wide, frames, per_group)
    stat_sq = group_totals(acts_wide * acts_wide, frames, per_group)
    stat_sum, stat_sq = lax.psum((stat_sum, stat_sq), "tile")
    group_mean = stat_sum / group_size
    inv_std = lax.rsqrt(stat_sq / group_size - group_mean * group_mean + norm_eps)
    mean_chan = jnp.repeat(group_mean, per_group, axis=1)[:, None, None, :]
    inv_chan = jnp.repeat(inv_std, per_group, axis=1)[:, None, None, :]
    normed = (acts_wide - mean_chan) * inv_chan
    shifted = normed * gamma + beta
    gate_value = jax.nn.sigmoid(shifted)
    hidden = (shifted * gate_value).astype(jnp.bfloat16)
    previous = from_behind(hidden, "block", 1)
    joined = jnp.concatenate([previous, hidden], 0)
    padded = padded_2(joined, (("tile", 1),), 1)
    upsampled = jnp.repeat(jnp.repeat(padded, 2, axis=1), 2, axis=2)[:, 1 : 2 * low_rows + 3]
    upsampled = jnp.pad(upsampled, ((0, 0), (0, 0), (1, 1), (0, 0)))
    following = from_behind(cotangent, "block", -1)
    grad_field = jnp.concatenate([cotangent, following], 0)
    grad_field = padded_2(grad_field, (("tile", 1),), 1)
    grad_field = jnp.pad(grad_field, ((0, 0), (0, 0), (1, 1), (0, 0)))
    up_rows = 2 * low_rows
    up_cols = 2 * low_cols
    num_cells = frames * up_rows * up_cols
    tap_list = [(tap // 9, tap // 3 % 3, tap % 3) for tap in range(27)]
    windows = [
        grad_field[
            2 - tap_t : 2 - tap_t + frames,
            2 - tap_h : 2 - tap_h + up_rows,
            2 - tap_w : 2 - tap_w + up_cols,
        ].reshape(num_cells, -1)
        for tap_t, tap_h, tap_w in tap_list
    ]
    columns = jnp.concatenate(windows, 1)
    piece_rows = lax.all_gather(weights, "tile", axis=0, tiled=True)
    flat_rows = piece_rows.reshape(piece_rows.shape[0], -1)
    back_grad = lax.dot_general(
        columns, flat_rows, (((1,), (1,)), ((), ())), preferred_element_type=jnp.float32
    )
    back_grad = back_grad.reshape(frames, low_rows, 2, low_cols, 2, piece_rows.shape[0])
    act_grad = back_grad.sum(axis=(2, 4))
    silu_slope = gate_value * (1.0 + shifted * (1.0 - gate_value))
    norm_grad = act_grad * silu_slope * gamma
    first_sum = group_totals(norm_grad, frames, per_group)
    second_sum = group_totals(norm_grad * normed, frames, per_group)
    first_sum, second_sum = lax.psum((first_sum, second_sum), "tile")
    first_chan = jnp.repeat(first_sum / group_size, per_group, axis=1)[:, None, None, :]
    second_chan = jnp.repeat(second_sum / group_size, per_group, axis=1)[:, None, None, :]
    d_acts = (inv_chan * (norm_grad - first_chan - normed * second_chan)).astype(jnp.bfloat16)
    flat_grads = cotangent.reshape(num_cells, -1)
    term_list = []
    for tap_t, tap_h, tap_w in tap_list:
        window_h = upsampled[
            tap_t : tap_t + frames, tap_h : tap_h + up_rows, tap_w : tap_w + up_cols
        ].reshape(num_cells, channels)
        term_list.append(
            lax.dot_general(
                window_h, flat_grads, (((0,), (0,)), ((), ())), preferred_element_type=jnp.float32
            )
        )
    whole_terms = jnp.stack(term_list, 1)
    whole_terms = lax.psum(whole_terms, "block")
    d_weights = lax.psum_scatter(whole_terms, "tile", scatter_dimension=0, tiled=True)
    return (d_acts, d_weights)


def solution(mesh):
    placed = (
        P("block", "tile", None, None),
        P(),
        P(),
        P("tile", None, None),
        P("block", "tile", None, None),
    )
    return jax.shard_map(
        shards,
        mesh=mesh,
        in_specs=placed,
        out_specs=(P("block", "tile", None, None), P("tile", None, None)),
        check_vma=False,
    )
```

profile of v0, /device:TPU:2, one launch (start us, length us, event | category | flops | bytes accessed | tf_op | source)
XLA Modules:
  0.0 430.7 jit_solution(1480891718286037013)
XLA Ops:
  11.7 56.1 %all-reduce.3 = (f32[2,32]{1,0:T(2,128)S(1)}, f32[2,32]{1,0:T(2,128)S(1)}) all-reduce(f32[2,32]{1,0:T(2,128)S(1)} %reduce_sum.86, f32[2,32]{1,0:T(2,128)S(1)} %reduce_sum.84), channel_id=1, replica_groups=mesh['block'=8,'tile'=32] {'tile'}, use_global_device_ids=true, to_apply=%region_5.0 | all-reduce | flops 128 | bytes 1024 | tf_op jit(solution)/shard_map/psum | solution.py:41
  68.8 1.9 collective-permute-start.1
  70.8 5.8 %collective-permute-start.2 = (bf16[4,1,128,192]{2,3,1,0:T(8,128)(2,1)S(1)}, bf16[4,1,128,192]{2,3,1,0:T(8,128)(2,1)S(1)}, u32[]{:S(2)}, u32[]{:S(2)}) collective-permute-start(bf16[4,1,128,192]{2,3,1,0:T(8,128)(2,1)S(1)} %get-tuple-element.44), channel_id=1, source_target_pairs={{1,0},{2,1},{3,2},{4,3},{5,4},{6,5},{7,6},{8,7},{9,8},{10,9},{11,1... | collective-permute-start | bytes 589832 | tf_op jit(solution)/shard_map/ppermute | solution.py:24
  77.9 1.8 collective-permute-done.2
  83.8 2.5 fusion.110
  88.0 1.8 copy.86
  90.8 1.8 copy.85
  92.6 1.7 copy.112
  94.3 1.8 copy.83
  96.1 1.7 copy.110
  97.7 1.8 copy.82
  99.5 1.7 copy.109
  101.2 1.8 copy.80
  103.0 1.7 copy.107
  104.7 1.8 copy.79
  106.5 1.7 copy.106
  108.2 1.8 copy.77
  110.0 1.7 copy.104
  111.7 1.8 copy.76
  113.5 1.7 copy.103
  115.2 1.8 copy.74
  117.0 1.7 copy.101
  118.7 1.8 copy.73
  120.5 1.7 copy.100
  122.1 1.8 copy.71
  123.9 1.7 copy.98
  125.6 1.8 copy.70
  127.4 1.7 copy.97
  129.1 1.8 copy.68
  132.5 1.8 copy.67
  134.3 1.7 copy.94
  136.0 1.8 copy.65
  137.8 1.7 copy.92
  139.5 9.7 %concatenate.111 = bf16[2,1,2,64,2,5184]{5,3,4,2,0,1:T(8,128)(2,1)} concatenate(bf16[2,1,2,64,2,192]{5,3,4,2,0,1:T(8,128)(2,1)} %copy.92, bf16[2,1,2,64,2,192]{5,3,4,2,0,1:T(8,128)(2,1)S(1)} %copy.93, bf16[2,1,2,64,2,192]{5,3,4,2,0,1:T(8,128)(2,1)} %copy.94, bf16[2,1,2,64,2,192]{5,3,4,2,0,1:T(8,128)(2,1)} %copy.95, bf16[2,1,2,64,2,192]{5,3,4,2,0,1:T(8,128)(2,1)S(1)} %copy.96, ...), dimensions={5} | concatenate | bytes 10616832 | tf_op jit(solution)/shard_map/concatenate | solution.py:71
  149.2 8.6 %copy.119 = bf16[384,27,192]{0,2,1:T(8,128)(2,1)} copy(bf16[384,27,192]{2,1,0:T(8,128)(2,1)} %all-gather.2.cloned.1.call-done) | data formatting | bytes 7962624 | tf_op jit(solution)/shard_map/all_gather | solution.py:72
  157.8 6.7 %fusion.8 = f32[2,64,384]{2,1,0:T(8,128)S(1)} fusion(bf16[384,5184,1,1,1]{0,1,4,3,2:T(8,128)(2,1)} %bitcast.286, bf16[2,1,2,64,2,5184]{5,3,4,2,0,1:T(8,128)(2,1)} %concatenate.111), kind=kOutput, calls=%fused_computation.10 | convolution fusion | flops 2038579200 | bytes 9486336 | tf_op jit(solution)/shard_map/dot_general | solution.py:74
  164.7 4.4 %collective-permute-start.3 = (bf16[2,1,64,384]{3,2,1,0:T(8,128)(2,1)S(1)}, bf16[2,1,64,384]{3,2,1,0:T(8,128)(2,1)S(1)}, u32[]{:S(2)}, u32[]{:S(2)}) collective-permute-start(bf16[2,1,64,384]{3,2,1,0:T(8,128)(2,1)S(1)} %get-tuple-element.45), channel_id=1, source_target_pairs={{0,32},{32,64},{64,96},{96,128},{128,160},{160,192},{192,224},{1,3... | collective-permute-start | bytes 294920 | tf_op jit(solution)/shard_map/ppermute | solution.py:13
  169.1 2.2 collective-permute-done.3
  171.3 5.1 %collective-permute-start.5 = (bf16[4,1,64,384]{3,2,1,0:T(8,128)(2,1)S(1)}, bf16[4,1,64,384]{3,2,1,0:T(8,128)(2,1)S(1)}, u32[]{:S(2)}, u32[]{:S(2)}) collective-permute-start(bf16[4,1,64,384]{3,2,1,0:T(8,128)(2,1)S(1)} %pad_maximum_fusion.3), channel_id=1, source_target_pairs={{1,0},{2,1},{3,2},{4,3},{5,4},{6,5},{7,6},{8,7},{9,8},{10,9},{11,1... | collective-permute-start | bytes 589832 | tf_op jit(solution)/shard_map/ppermute | solution.py:24
  176.4 2.1 collective-permute-start.4
  179.5 5.9 %collective-permute-done.4 = bf16[4,1,64,384]{3,2,1,0:T(8,128)(2,1)S(1)} collective-permute-done((bf16[4,1,64,384]{3,2,1,0:T(8,128)(2,1)S(1)}, bf16[4,1,64,384]{3,2,1,0:T(8,128)(2,1)S(1)}, u32[]{:S(2)}, u32[]{:S(2)}) %collective-permute-start.4) | collective-permute-done | bytes 196640 | tf_op jit(solution)/shard_map/ppermute | solution.py:23
  185.7 3.2 broadcast_in_dim.26
  188.9 5.1 %reshape.166 = bf16[4,6,128,384]{3,2,1,0:T(8,128)(2,1)S(1)} reshape(bf16[4,6,64,2,384]{4,3,2,1,0:T(2,128)(2,1)} %broadcast_in_dim.26) | data formatting | bytes 4718592 | tf_op jit(solution)/shard_map/reshape | solution.py:53
  220.9 12.0 %copy.120 = f32[384,27,192]{2,1,0:T(8,128)} copy(f32[384,27,192]{0,2,1:T(8,128)} %fusion.11) | data formatting | bytes 15925248 | tf_op jit(solution)/shard_map/stack | solution.py:98
  233.4 53.0 %all-reduce.2 = (f32[2,32]{1,0:T(2,128)S(1)}, f32[2,32]{1,0:T(2,128)S(1)}) all-reduce(f32[2,32]{1,0:T(2,128)S(1)} %reduce_sum.92, f32[2,32]{1,0:T(2,128)S(1)} %reduce_sum.90), channel_id=1, replica_groups=mesh['block'=8,'tile'=32] {'tile'}, use_global_device_ids=true, to_apply=%region_12.13 | all-reduce | flops 128 | bytes 1024 | tf_op jit(solution)/shard_map/psum | solution.py:83
  286.4 60.6 %reduce-scatter.2.cloned.1.call-done = f32[12,27,192]{2,1,0:T(8,128)} async-done(((f32[384,27,192]{2,1,0:T(8,128)}), f32[12,27,192]{2,1,0:T(8,128)}) %reduce-scatter.2.cloned.1.call-update) | async-done | bytes 248848 | tf_op jit(solution)/shard_map/reduce_scatter | solution.py:100
  348.1 74.3 %all-reduce.6.cloned.1.call-done = f32[12,27,192]{2,1,0:T(8,128)} async-done(((f32[12,27,192]{2,1,0:T(8,128)}), f32[12,27,192]{2,1,0:T(8,128)}) %all-reduce.6.cloned.1.call-update) | async-done | bytes 248848 | tf_op jit(solution)/shard_map/psum | solution.py:99
  422.4 1.8 copy.177
  (102 shorter events, 45.1 us)
Async XLA Ops:
  7.2 142.0 %all-gather.2.cloned.1.call-start = ((), (), s32[]{:S(2)}) async-start(), calls=%async_computation.1 | async-start | bytes 6488064 | tf_op jit(solution)/shard_map/all_gather | solution.py:72
  7.9 339.1 %reduce-scatter.2.cloned.1.call-start = ((), (), s32[]{:S(2)}) async-start(), calls=%async_computation.2 | async-start | bytes 12976128 | tf_op jit(solution)/shard_map/reduce_scatter | solution.py:100
  7.9 60.8 %collective-permute-start = (bf16[2,2,128,192]{2,3,1,0:T(8,128)(2,1)}, bf16[2,2,128,192]{2,3,1,0:T(8,128)(2,1)S(1)}, u32[]{:S(2)}, u32[]{:S(2)}) collective-permute-start(bf16[2,2,128,192]{2,3,1,0:T(8,128)(2,1)} %param.9), channel_id=1, source_target_pairs={{32,0},{64,32},{96,64},{128,96},{160,128},{192,160},{224,192},{33,... | collective-permute-start | bytes 589832 | tf_op jit(solution)/shard_map/ppermute | solution.py:13
  68.8 9.1 %collective-permute-start.1 = (bf16[4,1,128,192]{2,3,1,0:T(8,128)(2,1)S(1)}, bf16[4,1,128,192]{2,3,1,0:T(8,128)(2,1)S(1)}, u32[]{:S(2)}, u32[]{:S(2)}) collective-permute-start(bf16[4,1,128,192]{2,3,1,0:T(8,128)(2,1)S(1)} %get-tuple-element.43), channel_id=1, source_target_pairs={{0,1},{1,2},{2,3},{3,4},{4,5},{5,6},{6,7},{7,8},{8,9},{9,10},{10,1... | collective-permute-start | bytes 589832 | tf_op jit(solution)/shard_map/ppermute | solution.py:23
  70.8 8.9 %collective-permute-start.2 = (bf16[4,1,128,192]{2,3,1,0:T(8,128)(2,1)S(1)}, bf16[4,1,128,192]{2,3,1,0:T(8,128)(2,1)S(1)}, u32[]{:S(2)}, u32[]{:S(2)}) collective-permute-start(bf16[4,1,128,192]{2,3,1,0:T(8,128)(2,1)S(1)} %get-tuple-element.44), channel_id=1, source_target_pairs={{1,0},{2,1},{3,2},{4,3},{5,4},{6,5},{7,6},{8,7},{9,8},{10,9},{11,1... | collective-permute-start | bytes 589832 | tf_op jit(solution)/shard_map/ppermute | solution.py:24
  157.7 6.7 %copy-start.1 = (bf16[2,1,64,384]{3,2,1,0:T(8,128)(2,1)S(1)}, bf16[2,1,64,384]{3,2,1,0:T(8,128)(2,1)}, u32[]{:S(2)}) copy-start(bf16[2,1,64,384]{3,2,1,0:T(8,128)(2,1)} %param.5) | copy-start | bytes 294916
  157.7 6.7 %copy-start.2 = (f32[384]{0:T(512)S(1)}, f32[384]{0:T(512)}, u32[]{:S(2)}) copy-start(f32[384]{0:T(512)} %param.7) | copy-start | bytes 4612
  157.8 6.7 %copy-start.3 = (f32[384]{0:T(512)S(1)}, f32[384]{0:T(512)}, u32[]{:S(2)}) copy-start(f32[384]{0:T(512)} %param.6) | copy-start | bytes 4612
  164.7 6.6 %collective-permute-start.3 = (bf16[2,1,64,384]{3,2,1,0:T(8,128)(2,1)S(1)}, bf16[2,1,64,384]{3,2,1,0:T(8,128)(2,1)S(1)}, u32[]{:S(2)}, u32[]{:S(2)}) collective-permute-start(bf16[2,1,64,384]{3,2,1,0:T(8,128)(2,1)S(1)} %get-tuple-element.45), channel_id=1, source_target_pairs={{0,32},{32,64},{64,96},{96,128},{128,160},{160,192},{192,224},{1,3... | collective-permute-start | bytes 294920 | tf_op jit(solution)/shard_map/ppermute | solution.py:13
  171.3 8.2 %collective-permute-start.5 = (bf16[4,1,64,384]{3,2,1,0:T(8,128)(2,1)S(1)}, bf16[4,1,64,384]{3,2,1,0:T(8,128)(2,1)S(1)}, u32[]{:S(2)}, u32[]{:S(2)}) collective-permute-start(bf16[4,1,64,384]{3,2,1,0:T(8,128)(2,1)S(1)} %pad_maximum_fusion.3), channel_id=1, source_target_pairs={{1,0},{2,1},{3,2},{4,3},{5,4},{6,5},{7,6},{8,7},{9,8},{10,9},{11,1... | collective-permute-start | bytes 589832 | tf_op jit(solution)/shard_map/ppermute | solution.py:24
  176.4 9.1 %collective-permute-start.4 = (bf16[4,1,64,384]{3,2,1,0:T(8,128)(2,1)S(1)}, bf16[4,1,64,384]{3,2,1,0:T(8,128)(2,1)S(1)}, u32[]{:S(2)}, u32[]{:S(2)}) collective-permute-start(bf16[4,1,64,384]{3,2,1,0:T(8,128)(2,1)S(1)} %pad_maximum_fusion.3), channel_id=1, source_target_pairs={{0,1},{1,2},{2,3},{3,4},{4,5},{5,6},{6,7},{7,8},{8,9},{9,10},{10,1... | collective-permute-start | bytes 589832 | tf_op jit(solution)/shard_map/ppermute | solution.py:23
  188.9 5.3 %copy-start = (bf16[2,2,128,192]{2,3,1,0:T(8,128)(2,1)S(1)}, bf16[2,2,128,192]{2,3,1,0:T(8,128)(2,1)}, u32[]{:S(2)}) copy-start(bf16[2,2,128,192]{2,3,1,0:T(8,128)(2,1)} %param.9) | copy-start | bytes 589828
  232.9 189.4 %all-reduce.6.cloned.1.call-start = ((), (), s32[]{:S(2)}) async-start(), calls=%async_computation.3 | async-start | bytes 786432 | tf_op jit(solution)/shard_map/psum | solution.py:99
Sparse Core Ops, SparseCore 0:
  10.5 56.0 all-gather.1
  233.1 113.8 reduce-scatter.1
  349.3 72.9 all-reduce.5
where the time goes:
time: 433 us; the launch traced here: 431 us
  waiting for transfers between devices  147 us (34%)
  blocking collectives  109 us (25%)
  local copies, waits for them, and re-layouts  102 us (24%)
  matrix products  33.4 us (8%)
  starting transfers between devices  20.7 us (5%)
  between operations  14.2 us (3%)
    psum x1, waiting for transfers between devices, shards(): whole_terms = lax.psum(whole_terms, 'block')  74.3 us
    reduce_scatter x1, waiting for transfers between devices, shards(): lax.psum_scatter(whole_terms, 'tile', scatter_dimension=0, tiled=True)  60.6 us
    psum x1, blocking collectives, shards(): stat_sum, stat_sq = lax.psum((stat_sum, stat_sq), 'tile')  56.1 us
    psum x1, blocking collectives, shards(): first_sum, second_sum = lax.psum((first_sum, second_sum), 'tile')  53 us
    concatenate x28, local copies, waits for them, and re-layouts, shards(): columns = jnp.concatenate(windows, 1)  34.5 us
    slice x26, local copies, waits for them, and re-layouts, shards(): grad_field[2 - tap_t:2 - tap_t + frames, 2 - tap_h:2 - tap_h + up_rows, 2...  33.3 us
    dot_general x27, matrix products, shards(): lax.dot_general(window_h, flat_grads, (((0,), (0,)), ((), ())), preferred...  26.7 us
    another operation x1, local copies, waits for them, and re-layouts, shards(): whole_terms = jnp.stack(term_list, 1)  12 us
  transfers between devices with their start and end apart: 9, of which 7 were waited for; matrix products, arithmetic and copies ran while one was open for 17% of the time, Pallas kernels for 0%

commit v1 on v0

--- a/solution.py
+++ b/solution.py
@@ -96,7 +96,11 @@
             )
         )
     whole_terms = jnp.stack(term_list, 1)
-    whole_terms = lax.psum(whole_terms, "block")
+    whole_terms = whole_terms
+    for hop in (1, 2, 4):
+        whole_terms = whole_terms + lax.ppermute(
+            whole_terms, "block", [(dev, dev ^ hop) for dev in range(8)]
+        )
     d_weights = lax.psum_scatter(whole_terms, "tile", scatter_dimension=0, tiled=True)
     return (d_acts, d_weights)
 

time: 433 us -> 1220 us (2.82)
  waiting for transfers between devices: 147 us -> 912 us
  other arithmetic: 3.85 us -> 25 us
  matrix products: 33.4 us -> 14 us
  starting transfers between devices: 20.7 us -> 33.4 us
    ppermute x0 -> x3, waiting for transfers between devices: none -> 845 us  [shards(): lax.ppermute(whole_terms, 'block', [(dev, dev ^ hop) for dev in range(8)])]
    psum x1 -> x0, waiting for transfers between devices: 74.3 us -> none  [shards(): whole_terms = lax.psum(whole_terms, 'block')]
    add x0 -> x3, other arithmetic: none -> 21.2 us  [shards(): whole_terms + lax.ppermute(whole_terms, 'block', [(dev, dev ^ hop) for de...]
    dot_general x27, matrix products: 26.7 us -> 7.25 us  [shards(): lax.dot_general(window_h, flat_grads, (((0,), (0,)), ((), ())), preferred...]
    ppermute x0 -> x3, starting transfers between devices: none -> 12.8 us  [shards(): lax.ppermute(whole_terms, 'block', [(dev, dev ^ hop) for dev in range(8)])]
  transfers between devices with their start and end apart: 9 -> 11, of which waited for: 7 -> 9; matrix products, arithmetic and copies ran while one was open for 17% -> 6% of each run, Pallas kernels for 0% -> 0%
where the time goes in v1:
time: 1220 us
  waiting for transfers between devices  912 us (75%)
  blocking collectives  117 us (10%)
  local copies, waits for them, and re-layouts  101 us (8%)
  starting transfers between devices  33.4 us (3%)
  other arithmetic  25 us (2%)
  between operations  14.6 us (1%)
  matrix products  14 us (1%)
    ppermute x3, waiting for transfers between devices, shards(): lax.ppermute(whole_terms, 'block', [(dev, dev ^ hop) for dev in range(8)])  845 us
    psum x1, blocking collectives, shards(): first_sum, second_sum = lax.psum((first_sum, second_sum), 'tile')  60.8 us
    psum x1, blocking collectives, shards(): stat_sum, stat_sq = lax.psum((stat_sum, stat_sq), 'tile')  56.1 us
    reduce_scatter x1, waiting for transfers between devices, shards(): lax.psum_scatter(whole_terms, 'tile', scatter_dimension=0, tiled=True)  55.1 us
    concatenate x28, local copies, waits for them, and re-layouts, shards(): columns = jnp.concatenate(windows, 1)  34.5 us
    slice x26, local copies, waits for them, and re-layouts, shards(): grad_field[2 - tap_t:2 - tap_t + frames, 2 - tap_h:2 - tap_h + up_rows, 2...  33.3 us
  transfers between devices with their start and end apart: 11, of which 9 were waited for; matrix products, arithmetic and copies ran while one was open for 6% of the time, Pallas kernels for 0%

profile of v1, /device:TPU:2, one launch (start us, length us, event | category | flops | bytes accessed | tf_op | source)
XLA Modules:
  0.0 1217.3 jit_solution(319310215338063853)
XLA Ops:
  11.7 56.1 %all-reduce.3 = (f32[2,32]{1,0:T(2,128)S(1)}, f32[2,32]{1,0:T(2,128)S(1)}) all-reduce(f32[2,32]{1,0:T(2,128)S(1)} %reduce_sum.86, f32[2,32]{1,0:T(2,128)S(1)} %reduce_sum.84), channel_id=1, replica_groups=mesh['block'=8,'tile'=32] {'tile'}, use_global_device_ids=true, to_apply=%region_5.0 | all-reduce | flops 128 | bytes 1024 | tf_op jit(solution)/shard_map/psum | solution.py:41
  68.8 1.9 collective-permute-start.1
  70.8 5.8 collective-permute-start.2
  77.9 1.8 collective-permute-done.2
  83.8 2.5 fusion.110
  88.0 1.8 copy.86
  90.8 1.8 copy.85
  94.3 1.8 copy.83
  97.7 1.8 copy.82
  101.2 1.8 copy.80
  103.0 1.7 copy.107
  104.7 1.8 copy.79
  106.5 1.7 copy.106
  108.2 1.8 copy.77
  110.0 1.7 copy.104
  111.7 1.8 copy.76
  113.5 1.7 copy.103
  115.2 1.8 copy.74
  117.0 1.7 copy.101
  118.7 1.8 copy.73
  122.1 1.8 copy.71
  125.6 1.8 copy.70
  129.1 1.8 copy.68
  132.5 1.8 copy.67
  134.3 1.7 copy.94
  136.0 1.8 copy.65
  139.5 9.7 concatenate.111
  149.2 8.6 copy.119
  157.8 6.7 fusion.8
  164.7 4.4 collective-permute-start.3
  169.1 2.2 collective-permute-done.3
  171.3 5.1 collective-permute-start.5
  176.4 2.1 collective-permute-start.4
  179.5 5.9 collective-permute-done.4
  185.7 3.2 broadcast_in_dim.26
  188.9 5.1 reshape.166
  201.6 2.2 collective-permute-start.6
  204.7 165.0 %collective-permute-done.6 = f32[384,27,192]{0,2,1:T(8,128)} collective-permute-done((f32[384,27,192]{0,2,1:T(8,128)S(1)}, f32[384,27,192]{0,2,1:T(8,128)}, u32[]{:S(2)}, u32[]{:S(2)}) %collective-permute-start.6) | collective-permute-done | bytes 7962656 | tf_op jit(solution)/shard_map/ppermute | solution.py:101
  369.6 6.4 add.49
  376.0 4.4 collective-permute-start.7
  380.4 335.9 %collective-permute-done.7 = f32[384,27,192]{0,2,1:T(8,128)} collective-permute-done((f32[384,27,192]{0,2,1:T(8,128)S(1)}, f32[384,27,192]{0,2,1:T(8,128)}, u32[]{:S(2)}, u32[]{:S(2)}) %collective-permute-start.7) | collective-permute-done | bytes 7962656 | tf_op jit(solution)/shard_map/ppermute | solution.py:101
  716.3 7.4 add.50
  723.7 6.2 collective-permute-start.8
  730.0 343.7 %collective-permute-done.8 = f32[384,27,192]{0,2,1:T(8,128)S(1)} collective-permute-done((f32[384,27,192]{0,2,1:T(8,128)}, f32[384,27,192]{0,2,1:T(8,128)S(1)}, u32[]{:S(2)}, u32[]{:S(2)}) %collective-permute-start.8) | collective-permute-done | bytes 7962656 | tf_op jit(solution)/shard_map/ppermute | solution.py:101
  1073.7 7.4 add.51
  1081.1 12.0 copy.120
  1093.5 60.8 %all-reduce.2 = (f32[2,32]{1,0:T(2,128)S(1)}, f32[2,32]{1,0:T(2,128)S(1)}) all-reduce(f32[2,32]{1,0:T(2,128)S(1)} %reduce_sum.92, f32[2,32]{1,0:T(2,128)S(1)} %reduce_sum.90), channel_id=1, replica_groups=mesh['block'=8,'tile'=32] {'tile'}, use_global_device_ids=true, to_apply=%region_12.13 | all-reduce | flops 128 | bytes 1024 | tf_op jit(solution)/shard_map/psum | solution.py:83
  1155.4 55.1 %reduce-scatter.2.cloned.1.call-done = f32[12,27,192]{2,1,0:T(8,128)} async-done(((f32[384,27,192]{2,1,0:T(8,128)}), f32[12,27,192]{2,1,0:T(8,128)}) %reduce-scatter.2.cloned.1.call-update) | async-done | bytes 248848 | tf_op jit(solution)/shard_map/reduce_scatter | solution.py:104
  (109 shorter events, 38.1 us)
Async XLA Ops:
  7.2 142.0 %all-gather.2.cloned.1.call-start = ((), (), s32[]{:S(2)}) async-start(), calls=%async_computation.1 | async-start | bytes 6488064 | tf_op jit(solution)/shard_map/all_gather | solution.py:72
  7.9 1202.6 %reduce-scatter.2.cloned.1.call-start = ((), (), s32[]{:S(2)}) async-start(), calls=%async_computation.2 | async-start | bytes 12976128 | tf_op jit(solution)/shard_map/reduce_scatter | solution.py:104
  7.9 60.8 %collective-permute-start = (bf16[2,2,128,192]{2,3,1,0:T(8,128)(2,1)}, bf16[2,2,128,192]{2,3,1,0:T(8,128)(2,1)S(1)}, u32[]{:S(2)}, u32[]{:S(2)}) collective-permute-start(bf16[2,2,128,192]{2,3,1,0:T(8,128)(2,1)} %param.9), channel_id=1, source_target_pairs={{32,0},{64,32},{96,64},{128,96},{160,128},{192,160},{224,192},{33,... | collective-permute-start | bytes 589832 | tf_op jit(solution)/shard_map/ppermute | solution.py:13
  68.8 9.1 collective-permute-start.1
  70.8 8.9 collective-permute-start.2
  157.7 6.7 copy-start.2
  157.7 6.7 copy-start.3
  157.8 6.7 copy-start.4
  164.7 6.6 collective-permute-start.3
  171.3 8.2 collective-permute-start.5
  176.4 9.1 collective-permute-start.4
  188.9 5.3 copy-start
  201.6 3.1 copy-start.1
  201.6 168.1 %collective-permute-start.6 = (f32[384,27,192]{0,2,1:T(8,128)S(1)}, f32[384,27,192]{0,2,1:T(8,128)}, u32[]{:S(2)}, u32[]{:S(2)}) collective-permute-start(f32[384,27,192]{0,2,1:T(8,128)S(1)} %fusion.11), channel_id=1, source_target_pairs={{0,32},{32,0},{64,96},{96,64},{128,160},{160,128},{192,224},{224,1... | collective-permute-start | bytes 23887880 | tf_op jit(solution)/shard_map/ppermute | solution.py:101
  376.0 340.3 %collective-permute-start.7 = (f32[384,27,192]{0,2,1:T(8,128)S(1)}, f32[384,27,192]{0,2,1:T(8,128)}, u32[]{:S(2)}, u32[]{:S(2)}) collective-permute-start(f32[384,27,192]{0,2,1:T(8,128)S(1)} %add.49), channel_id=1, source_target_pairs={{0,64},{32,96},{64,0},{96,32},{128,192},{160,224},{192,128},{224,1... | collective-permute-start | bytes 23887880 | tf_op jit(solution)/shard_map/ppermute | solution.py:101
  723.7 350.0 %collective-permute-start.8 = (f32[384,27,192]{0,2,1:T(8,128)}, f32[384,27,192]{0,2,1:T(8,128)S(1)}, u32[]{:S(2)}, u32[]{:S(2)}) collective-permute-start(f32[384,27,192]{0,2,1:T(8,128)} %add.50), channel_id=1, source_target_pairs={{0,128},{32,160},{64,192},{96,224},{128,0},{160,32},{192,64},{224,... | collective-permute-start | bytes 23887880 | tf_op jit(solution)/shard_map/ppermute | solution.py:101
Sparse Core Ops, SparseCore 0:
  10.5 56.0 all-gather.1
  1093.2 117.2 reduce-scatter.1
